TPU v7x, 128 devices: a whole 4x4x4 slice. The times are simulated.
128 devices in a mesh: row: 8 (over z, x_lo), col: 16 (over x_hi, y, core).
Axes of the slice: x: 4 (x_hi: 2, x_lo: 2; x = x_hi * 2 + x_lo), y: 4, z: 4, core: 2. Of those that a mesh axis runs over, the one named last changes fastest.
Arguments:
- blocks: bfloat16 [8, 16, 192, 128, 128], P('row', 'col'), may hold values from -0.059814453 to 0.059814453
- block_rows: int32 [8, 16, 192], P('row', 'col'), may hold values from 0 to 255, as said below
- block_cols: int32 [8, 16, 192], P('row', 'col'), may hold values from 0 to 255, as said below
- counts: int32 [8, 16], P('row', 'col'), may hold values from 96 to 192, as said below
- travel_times: float32 [16, 262144], P(None, ('row', 'col')), may hold values from -6 to 6
Outputs:
- solution: float32 [16, 16, 8, 4096], P(None, 'col', 'row')
- scaled_direction: float32 [16, 16, 8, 4096], P(None, 'col', 'row')
Inputs may be any that keep to these rules, and one draw needn't show every extreme that they name: Ray block of a slot within the 256 ray blocks of its row group; among the filled slots of one device the (block_rows, block_cols) pairs are all different. `block_cols`: cell block of a slot within the 256 cell blocks of its column group. `counts`: some device fills all 192 slots.
All inputs are finite; a program needn't handle non-finite values.
Results may differ from a plain program's by a relative error of at most 0.0054.
Values may be sent and summed in bfloat16 or wider, within the bound.
No kernel may reach another device: no remote copies, remote signals or barrier semaphores. Data moves between devices by JAX's collectives and lax.ppermute only.
A program may use at most 64 MiB of HBM per device.

v0:
```python
import jax
import jax.numpy as jnp
from jax import lax
from jax.sharding import PartitionSpec as P

RB_DEV = 256
CB_DEV = 256
ITERS = 2
norm_eps = 1e-06


def rotation(rho_bar, phi_bar, beta_norm, alpha_norm):
    rho_new = jnp.sqrt(rho_bar * rho_bar + beta_norm * beta_norm)
    cosine = rho_bar / rho_new
    sine_val = beta_norm / rho_new
    theta_coef = sine_val * alpha_norm
    rho_next = -cosine * alpha_norm
    phi_new = cosine * phi_bar
    phi_next = sine_val * phi_bar
    return (phi_new / rho_new, theta_coef / rho_new, rho_next, phi_next)


def forward_rows(right_full, blocks_here, cols_here, row_hot):
    count_rhs = right_full.shape[0]
    block_size = blocks_here.shape[1]
    cells = right_full.reshape(count_rhs, right_full.shape[1] // block_size, block_size)
    picked = jnp.take(cells, cols_here, axis=1)
    product = jnp.einsum("knj,nij->kni", picked, blocks_here, preferred_element_type=jnp.float32)
    summed = jnp.einsum("rn,kni->kri", row_hot, product, precision=lax.Precision.HIGHEST)
    return summed.reshape(count_rhs, -1)


def backward_cols(left_full, blocks_here, rows_here, col_hot):
    count_rhs = left_full.shape[0]
    block_size = blocks_here.shape[1]
    rays = left_full.reshape(count_rhs, left_full.shape[1] // block_size, block_size)
    picked = jnp.take(rays, rows_here, axis=1)
    product = jnp.einsum("kni,nij->knj", picked, blocks_here, preferred_element_type=jnp.float32)
    summed = jnp.einsum("cn,knj->kcj", col_hot, product, precision=lax.Precision.HIGHEST)
    return summed.reshape(count_rhs, -1)


def square_sums(values):
    return jnp.sum(values * values, axis=1)


def shards(blocks, block_rows, block_cols, counts, travel_times):
    blocks_here = blocks[0, 0]
    rows_here = block_rows[0, 0]
    cols_here = block_cols[0, 0]
    slots = jnp.arange(blocks_here.shape[0], dtype=jnp.int32)
    filled = slots < counts[0, 0]
    row_hot = (
        (rows_here[None, :] == jnp.arange(RB_DEV, dtype=jnp.int32)[:, None]) & filled[None, :]
    ).astype(jnp.float32)
    col_hot = (
        (cols_here[None, :] == jnp.arange(CB_DEV, dtype=jnp.int32)[:, None]) & filled[None, :]
    ).astype(jnp.float32)
    count_rhs = travel_times.shape[0]

    def global_norm(partial_value):
        return jnp.sqrt(lax.psum(square_sums(partial_value), ("row", "col")) + norm_eps)

    def ray_side(partial_value):
        beta_norm = global_norm(partial_value)
        left_full = lax.all_gather(
            (partial_value / beta_norm[:, None]).astype(jnp.bfloat16), "col", axis=1, tiled=True
        )
        return (partial_value / beta_norm[:, None], left_full, beta_norm)

    def cell_side(partial_value):
        alpha_norm = global_norm(partial_value)
        right_full = None
        return (partial_value / alpha_norm[:, None], right_full, alpha_norm)

    def rows_to_cells(left_full):
        partial_value = backward_cols(left_full, blocks_here, rows_here, col_hot)
        return lax.psum_scatter(partial_value, "row", scatter_dimension=1, tiled=True)

    left_vec, left_full, beta_norm = ray_side(travel_times)
    right_vec, right_full, alpha_norm = cell_side(rows_to_cells(left_full))
    direction = right_vec
    solution = jnp.zeros_like(right_vec)
    phi_bar = beta_norm
    rho_bar = alpha_norm
    for iteration in range(ITERS):
        cells_right_full = lax.all_gather(right_vec.astype(jnp.bfloat16), "row", axis=1, tiled=True)
        cells_partial_value = forward_rows(cells_right_full, blocks_here, cols_here, row_hot)
        left_vec, left_full, beta_norm = ray_side(
            lax.psum_scatter(cells_partial_value, "col", scatter_dimension=1, tiled=True)
            - alpha_norm[:, None] * left_vec
        )
        right_vec, right_full, alpha_norm = cell_side(
            rows_to_cells(left_full) - beta_norm[:, None] * right_vec
        )
        step_scale, turn_scale, rho_bar, phi_bar = rotation(rho_bar, phi_bar, beta_norm, alpha_norm)
        solution = solution + step_scale[:, None] * direction
        direction = right_vec - turn_scale[:, None] * direction
    scaled = phi_bar[:, None] * direction
    return (solution.reshape(count_rhs, 1, 1, -1), scaled.reshape(count_rhs, 1, 1, -1))


def solution(mesh):
    placed = (
        P("row", "col", None, None, None),
        P("row", "col", None),
        P("row", "col", None),
        P("row", "col"),
        P(None, ("row", "col")),
    )
    return jax.shard_map(
        shards,
        mesh=mesh,
        in_specs=placed,
        out_specs=(P(None, "col", "row", None), P(None, "col", "row", None)),
        check_vma=False,
    )
```

profile of v0, /device:TPU:1, one launch (start us, length us, event | category | flops | bytes accessed | tf_op | source)
XLA Modules:
  0.0 989.8 jit_solution(17914631215639586107)
XLA Ops:
  7.2 1.0 multiply_reduce_fusion.5
  8.2 68.7 %psum.42 = f32[16]{0:T(128)S(1)} all-reduce(f32[16]{0:T(128)S(1)} %multiply_reduce_fusion.5), channel_id=1, replica_groups=mesh['row'=8,'col'=16] {'row','col'}, use_global_device_ids=true, to_apply=%region_1.0 | all-reduce | flops 16 | bytes 128 | tf_op jit(solution)/shard_map/psum | solution.py:62
  76.9 1.6 fusion.69
  79.3 0.7 compare_select_fusion.1
  80.0 0.7 compare_and_fusion.1
  80.7 39.5 %all-gather.6.cloned.1.call-done = bf16[16,32768]{1,0:T(8,128)(2,1)} async-done(((bf16[16,2048]{1,0:T(8,128)(2,1)}), bf16[16,32768]{1,0:T(8,128)(2,1)}) %all-gather.6.cloned.1.call-update) | async-done | bytes 1048592 | tf_op jit(solution)/shard_map/all_gather | solution.py:66
  120.1 1.4 copy_bitcast_fusion.9
  121.5 0.8 gather_fusion
  122.3 3.9 fusion.15
  126.3 2.0 convolution_bitcast_fusion.4
  128.2 1.8 copy.16
  130.1 4.2 copy.65
  134.3 51.0 %reduce-scatter.6.cloned.1.call-done = f32[16,4096]{1,0:T(8,128)} async-done(((f32[16,32768]{1,0:T(8,128)}), f32[16,4096]{1,0:T(8,128)}) %reduce-scatter.6.cloned.1.call-update) | async-done | bytes 262160 | tf_op jit(solution)/shard_map/reduce_scatter | solution.py:78
  185.3 1.1 multiply_reduce_fusion.2
  186.4 64.5 %psum.43 = f32[16]{0:T(128)S(1)} all-reduce(f32[16]{0:T(128)S(1)} %multiply_reduce_fusion.2), channel_id=1, replica_groups=mesh['row'=8,'col'=16] {'row','col'}, use_global_device_ids=true, to_apply=%region_4.6 | all-reduce | flops 16 | bytes 128 | tf_op jit(solution)/shard_map/psum | solution.py:62
  250.9 1.7 fusion.79
  252.7 0.2 reduce-scatter.8.cloned.1.call-start
  252.9 32.9 %all-gather.8.cloned.1.call-done = bf16[16,32768]{1,0:T(8,128)(2,1)} async-done(((bf16[16,4096]{1,0:T(8,128)(2,1)}), bf16[16,32768]{1,0:T(8,128)(2,1)}) %all-gather.8.cloned.1.call-update) | async-done | bytes 1048592 | tf_op jit(solution)/shard_map/all_gather | solution.py:87
  285.8 1.4 copy_bitcast_fusion.8
  287.2 0.8 gather_fusion.1
  288.0 5.5 fusion.18
  293.5 2.0 convolution_bitcast_fusion.3
  295.5 1.8 copy.19
  297.3 4.2 copy.64
  301.6 73.0 %reduce-scatter.8.cloned.1.call-done = f32[16,2048]{1,0:T(8,128)} async-done(((f32[16,32768]{1,0:T(8,128)}), f32[16,2048]{1,0:T(8,128)}) %reduce-scatter.8.cloned.1.call-update) | async-done | bytes 131088 | tf_op jit(solution)/shard_map/reduce_scatter | solution.py:90
  374.6 1.1 multiply_reduce_fusion.4
  375.7 66.4 %psum.44 = f32[16]{0:T(128)S(1)} all-reduce(f32[16]{0:T(128)S(1)} %get-tuple-element.17), channel_id=1, replica_groups=mesh['row'=8,'col'=16] {'row','col'}, use_global_device_ids=true, to_apply=%region_7.9 | all-reduce | flops 16 | bytes 128 | tf_op jit(solution)/shard_map/psum | solution.py:62
  442.1 0.7 fusion.70
  442.9 41.6 %all-gather.10.cloned.1.call-done = bf16[16,32768]{1,0:T(8,128)(2,1)} async-done(((bf16[16,2048]{1,0:T(8,128)(2,1)}), bf16[16,32768]{1,0:T(8,128)(2,1)}) %all-gather.10.cloned.1.call-update) | async-done | bytes 1048592 | tf_op jit(solution)/shard_map/all_gather | solution.py:66
  484.5 1.4 copy_bitcast_fusion.7
  485.9 0.8 gather_fusion.2
  486.7 3.9 fusion.21
  490.6 2.0 convolution_bitcast_fusion.2
  492.6 1.8 copy.22
  494.4 4.2 copy.63
  498.6 51.0 %reduce-scatter.10.cloned.1.call-done = f32[16,4096]{1,0:T(8,128)} async-done(((f32[16,32768]{1,0:T(8,128)}), f32[16,4096]{1,0:T(8,128)}) %reduce-scatter.10.cloned.1.call-update) | async-done | bytes 262160 | tf_op jit(solution)/shard_map/reduce_scatter | solution.py:78
  549.6 1.2 multiply_reduce_fusion.1
  550.8 64.8 %psum.45 = f32[16]{0:T(128)S(1)} all-reduce(f32[16]{0:T(128)S(1)} %multiply_reduce_fusion.1), channel_id=1, replica_groups=mesh['row'=8,'col'=16] {'row','col'}, use_global_device_ids=true, to_apply=%region_10.12 | all-reduce | flops 16 | bytes 128 | tf_op jit(solution)/shard_map/psum | solution.py:62
  615.6 1.7 fusion.83
  617.4 33.1 %all-gather.12.cloned.1.call-done = bf16[16,32768]{1,0:T(8,128)(2,1)} async-done(((bf16[16,4096]{1,0:T(8,128)(2,1)}), bf16[16,32768]{1,0:T(8,128)(2,1)}) %all-gather.12.cloned.1.call-update) | async-done | bytes 1048592 | tf_op jit(solution)/shard_map/all_gather | solution.py:87
  650.5 1.4 copy_bitcast_fusion.6
  651.9 0.8 gather_fusion.3
  652.7 5.5 fusion.24
  658.2 2.0 convolution_bitcast_fusion.1
  660.2 1.8 copy.25
  662.0 4.2 copy.62
  666.2 73.0 %reduce-scatter.12.cloned.1.call-done = f32[16,2048]{1,0:T(8,128)} async-done(((f32[16,32768]{1,0:T(8,128)}), f32[16,2048]{1,0:T(8,128)}) %reduce-scatter.12.cloned.1.call-update) | async-done | bytes 131088 | tf_op jit(solution)/shard_map/reduce_scatter | solution.py:90
  739.2 1.1 multiply_reduce_fusion.3
  740.3 66.4 %psum.46 = f32[16]{0:T(128)S(1)} all-reduce(f32[16]{0:T(128)S(1)} %get-tuple-element.13), channel_id=1, replica_groups=mesh['row'=8,'col'=16] {'row','col'}, use_global_device_ids=true, to_apply=%region_13.15 | all-reduce | flops 16 | bytes 128 | tf_op jit(solution)/shard_map/psum | solution.py:62
  806.8 0.7 divide_convert_fusion
  807.5 0.3 reduce-scatter.14.cloned.1.call-start
  807.8 41.2 %all-gather.14.cloned.1.call-done = bf16[16,32768]{1,0:T(8,128)(2,1)} async-done(((bf16[16,2048]{1,0:T(8,128)(2,1)}), bf16[16,32768]{1,0:T(8,128)(2,1)}) %all-gather.14.cloned.1.call-update) | async-done | bytes 1048592 | tf_op jit(solution)/shard_map/all_gather | solution.py:66
  849.0 1.4 copy_bitcast_fusion.5
  850.5 0.8 gather_fusion.4
  851.2 3.9 fusion.27
  855.1 2.0 convolution_bitcast_fusion
  857.1 1.8 copy.28
  859.0 4.2 copy.61
  863.1 51.1 %reduce-scatter.14.cloned.1.call-done = f32[16,4096]{1,0:T(8,128)} async-done(((f32[16,32768]{1,0:T(8,128)}), f32[16,4096]{1,0:T(8,128)}) %reduce-scatter.14.cloned.1.call-update) | async-done | bytes 262160 | tf_op jit(solution)/shard_map/reduce_scatter | solution.py:78
  914.2 1.2 multiply_reduce_fusion
  915.4 64.5 %psum.47 = f32[16]{0:T(128)S(1)} all-reduce(f32[16]{0:T(128)S(1)} %multiply_reduce_fusion), channel_id=1, replica_groups=mesh['row'=8,'col'=16] {'row','col'}, use_global_device_ids=true, to_apply=%region_16.18 | all-reduce | flops 16 | bytes 128 | tf_op jit(solution)/shard_map/psum | solution.py:62
  979.9 1.1 multiply_bitcast_fusion
  981.0 1.0 copy.30
  982.0 1.0 copy.29
  (37 shorter events, 0.6 us)
Async XLA Ops:
  7.2 113.0 %all-gather.6.cloned.1.call-start = ((), (), s32[]{:S(2)}) async-start(), calls=%async_computation.5 | async-start | bytes 1114112 | tf_op jit(solution)/shard_map/all_gather | solution.py:66
  78.6 106.7 %reduce-scatter.6.cloned.1.call-start = ((), (), s32[]{:S(2)}) async-start(), calls=%async_computation.6 | async-start | bytes 2359296 | tf_op jit(solution)/shard_map/reduce_scatter | solution.py:78
  122.3 3.9 copy-start.2
  134.3 151.6 %all-gather.8.cloned.1.call-start = ((), (), s32[]{:S(2)}) async-start(), calls=%async_computation.7 | async-start | bytes 1179648 | tf_op jit(solution)/shard_map/all_gather | solution.py:87
  252.7 121.9 %reduce-scatter.8.cloned.1.call-start = ((), (), s32[]{:S(2)}) async-start(), calls=%async_computation.8 | async-start | bytes 2228224 | tf_op jit(solution)/shard_map/reduce_scatter | solution.py:90
  288.0 5.5 copy-start.3
  301.5 73.1 %copy-start.1 = (f32[16,2048]{1,0:T(8,128)S(1)}, f32[16,2048]{1,0:T(8,128)}, u32[]{:S(2)}) copy-start(f32[16,2048]{1,0:T(8,128)} %param.11) | copy-start | bytes 393220
  301.5 183.0 %all-gather.10.cloned.1.call-start = ((), (), s32[]{:S(2)}) async-start(), calls=%async_computation.9 | async-start | bytes 1114112 | tf_op jit(solution)/shard_map/all_gather | solution.py:66
  442.9 106.8 %reduce-scatter.10.cloned.1.call-start = ((), (), s32[]{:S(2)}) async-start(), calls=%async_computation.10 | async-start | bytes 2359296 | tf_op jit(solution)/shard_map/reduce_scatter | solution.py:78
  498.6 51.1 %copy-start = (f32[16,4096]{1,0:T(8,128)S(1)}, f32[16,4096]{1,0:T(8,128)}, u32[]{:S(2)}) copy-start(f32[16,4096]{1,0:T(8,128)} %reduce-scatter.6.cloned.1.call-done) | copy-start | bytes 786436
  498.6 151.9 %all-gather.12.cloned.1.call-start = ((), (), s32[]{:S(2)}) async-start(), calls=%async_computation.11 | async-start | bytes 1179648 | tf_op jit(solution)/shard_map/all_gather | solution.py:87
  617.3 121.9 %reduce-scatter.12.cloned.1.call-start = ((), (), s32[]{:S(2)}) async-start(), calls=%async_computation.12 | async-start | bytes 2228224 | tf_op jit(solution)/shard_map/reduce_scatter | solution.py:90
  666.2 182.9 %all-gather.14.cloned.1.call-start = ((), (), s32[]{:S(2)}) async-start(), calls=%async_computation.13 | async-start | bytes 1114112 | tf_op jit(solution)/shard_map/all_gather | solution.py:66
  807.5 106.7 %reduce-scatter.14.cloned.1.call-start = ((), (), s32[]{:S(2)}) async-start(), calls=%async_computation.14 | async-start | bytes 2359296 | tf_op jit(solution)/shard_map/reduce_scatter | solution.py:78
Sparse Core Ops, SparseCore 0:
  78.7 41.3 all-gather.5
  134.4 50.8 reduce-scatter.5
  252.8 32.9 all-gather.7
  301.7 72.8 reduce-scatter.7
  443.0 41.4 all-gather.9
  498.7 50.8 reduce-scatter.9
  617.4 32.9 all-gather.11
  666.3 72.8 reduce-scatter.11
  807.6 41.3 all-gather.13
  863.3 50.8 reduce-scatter.13
where the time goes:
time: 991 us; the launch traced here: 990 us
  waiting for transfers between devices  487 us (49%)
  blocking collectives  395 us (40%)
  local copies, waits for them, and re-layouts  42.8 us (4%)
  matrix products  32.6 us (3%)
  other arithmetic  15.8 us (2%)
  between operations  15 us (2%)
    psum x6, blocking collectives, global_norm(): lax.psum(square_sums(partial_value), ('row', 'col')) + norm_eps  395 us
    reduce_scatter x3, waiting for transfers between devices, rows_to_cells(): lax.psum_scatter(partial_value, 'row', scatter_dimension=1, tiled=True)  153 us
    reduce_scatter x2, waiting for transfers between devices, shards(): lax.psum_scatter(cells_partial_value, 'col', scatter_dimension=1, tiled=T...  146 us
    all_gather x3, waiting for transfers between devices, ray_side(): lax.all_gather((partial_value / beta_norm[:, None]).astype(jnp.bfloat16),...  122 us
    all_gather x2, waiting for transfers between devices, shards(): lax.all_gather(right_vec.astype(jnp.bfloat16), 'row', axis=1, tiled=True)  66 us
    unnamed x15, local copies, waits for them, and re-layouts  22.8 us
  transfers between devices with their start and end apart: 10, of which 10 were waited for; matrix products, arithmetic and copies ran while one was open for 0% of the time, Pallas kernels for 0%

commit v1 on v0

--- a/solution.py
+++ b/solution.py
@@ -63,8 +63,17 @@
 
     def ray_side(partial_value):
         beta_norm = global_norm(partial_value)
-        left_full = lax.all_gather(
-            (partial_value / beta_norm[:, None]).astype(jnp.bfloat16), "col", axis=1, tiled=True
+        left_full = jnp.concatenate(
+            lax.all_to_all(
+                jnp.stack(
+                    [(partial_value / beta_norm[:, None]).astype(jnp.bfloat16)]
+                    * lax.axis_size("col")
+                ),
+                "col",
+                0,
+                0,
+            ),
+            axis=1,
         )
         return (partial_value / beta_norm[:, None], left_full, beta_norm)
 

time: 991 us -> 931 us (0.939)
  waiting for transfers between devices: 487 us -> 374 us
  blocking collectives: 395 us -> 438 us
    all_gather x3 -> x0, waiting for transfers between devices: 122 us -> none  [ray_side(): lax.all_gather((partial_value / beta_norm[:, None]).astype(jnp.bfloat16),...]
    all_to_all x0 -> x2, blocking collectives: none -> 42.4 us  [ray_side(): lax.all_to_all(jnp.stack([(partial_value / beta_norm[:, None]).astype(jnp...]
    all_to_all x0 -> x1, waiting for transfers between devices: none -> 16.3 us  [ray_side(): lax.all_to_all(jnp.stack([(partial_value / beta_norm[:, None]).astype(jnp...]
  transfers between devices with their start and end apart: 10 -> 8, of which waited for: 10 -> 8; matrix products, arithmetic and copies ran while one was open for 0% -> 0% of each run, Pallas kernels for 0% -> 0%
where the time goes in v1:
time: 931 us; the launch traced here: 923 us
  blocking collectives  438 us (47%)
  waiting for transfers between devices  374 us (40%)
  local copies, waits for them, and re-layouts  45.2 us (5%)
  matrix products  32.6 us (4%)
  between operations  15.3 us (2%)
  other arithmetic  12.5 us (1%)
    psum x6, blocking collectives, global_norm(): lax.psum(square_sums(partial_value), ('row', 'col')) + norm_eps  395 us
    reduce_scatter x2, waiting for transfers between devices, shards(): lax.psum_scatter(cells_partial_value, 'col', scatter_dimension=1, tiled=T...  146 us
    reduce_scatter x3, waiting for transfers between devices, rows_to_cells(): lax.psum_scatter(partial_value, 'row', scatter_dimension=1, tiled=True)  146 us
    all_gather x2, waiting for transfers between devices, shards(): lax.all_gather(right_vec.astype(jnp.bfloat16), 'row', axis=1, tiled=True)  65.7 us
    all_to_all x2, blocking collectives, ray_side(): lax.all_to_all(jnp.stack([(partial_value / beta_norm[:, None]).astype(jnp...  42.4 us
    unnamed x15, local copies, waits for them, and re-layouts  22.8 us
  transfers between devices with their start and end apart: 8, of which 8 were waited for; matrix products, arithmetic and copies ran while one was open for 0% of the time, Pallas kernels for 0%

profile of v1, /device:TPU:1, one launch (start us, length us, event | category | flops | bytes accessed | tf_op | source)
XLA Modules:
  0.0 922.5 jit_solution(2914508300123432339)
XLA Ops:
  7.2 1.0 multiply_reduce_fusion.5
  8.2 68.7 %psum.42 = f32[16]{0:T(128)S(1)} all-reduce(f32[16]{0:T(128)S(1)} %multiply_reduce_fusion.5), channel_id=1, replica_groups=mesh['row'=8,'col'=16] {'row','col'}, use_global_device_ids=true, to_apply=%region_1.0 | all-reduce | flops 16 | bytes 128 | tf_op jit(solution)/shard_map/psum | solution.py:62
  76.9 1.0 fusion.69
  77.9 1.1 stack.6
  79.0 4.8 all-to-all-start
  84.6 16.3 %all-to-all-done = bf16[16,16,2048]{2,1,0:T(8,128)(2,1)S(1)} async-done(((bf16[16,16,2048]{2,1,0:T(8,128)(2,1)}), bf16[16,16,2048]{2,1,0:T(8,128)(2,1)S(1)}, u32[]{:S(2)}, u32[]{:S(2)}) %all-to-all-start) | async-done | bytes 1048608 | tf_op jit(solution)/shard_map/all_to_all | solution.py:67
  100.9 0.6 copy.34
  102.0 0.7 copy.35
  102.7 0.8 gather_fusion
  103.5 3.9 fusion.15
  107.4 2.0 convolution_bitcast_fusion.4
  109.4 1.8 copy.37
  111.2 4.2 copy.82
  115.5 48.2 %reduce-scatter.6.cloned.1.call-done = f32[16,4096]{1,0:T(8,128)} async-done(((f32[16,32768]{1,0:T(8,128)}), f32[16,4096]{1,0:T(8,128)}) %reduce-scatter.6.cloned.1.call-update) | async-done | bytes 262160 | tf_op jit(solution)/shard_map/reduce_scatter | solution.py:87
  163.7 1.1 multiply_reduce_fusion.2
  164.8 64.6 %psum.43 = f32[16]{0:T(128)S(1)} all-reduce(f32[16]{0:T(128)S(1)} %multiply_reduce_fusion.2), channel_id=1, replica_groups=mesh['row'=8,'col'=16] {'row','col'}, use_global_device_ids=true, to_apply=%region_4.6 | all-reduce | flops 16 | bytes 128 | tf_op jit(solution)/shard_map/psum | solution.py:62
  229.4 1.7 fusion.79
  231.5 32.8 %all-gather.3.cloned.1.call-done = bf16[16,32768]{1,0:T(8,128)(2,1)} async-done(((bf16[16,4096]{1,0:T(8,128)(2,1)}), bf16[16,32768]{1,0:T(8,128)(2,1)}) %all-gather.3.cloned.1.call-update) | async-done | bytes 1048592 | tf_op jit(solution)/shard_map/all_gather | solution.py:96
  264.2 1.4 copy_bitcast_fusion.6
  265.6 0.8 gather_fusion.1
  266.4 5.5 fusion.18
  271.9 2.0 convolution_bitcast_fusion.3
  273.9 1.8 copy.40
  275.7 4.2 copy.81
  280.0 73.0 %reduce-scatter.8.cloned.1.call-done = f32[16,2048]{1,0:T(8,128)} async-done(((f32[16,32768]{1,0:T(8,128)}), f32[16,2048]{1,0:T(8,128)}) %reduce-scatter.8.cloned.1.call-update) | async-done | bytes 131088 | tf_op jit(solution)/shard_map/reduce_scatter | solution.py:99
  353.0 1.1 multiply_reduce_fusion.4
  354.1 66.4 %psum.44 = f32[16]{0:T(128)S(1)} all-reduce(f32[16]{0:T(128)S(1)} %get-tuple-element.19), channel_id=1, replica_groups=mesh['row'=8,'col'=16] {'row','col'}, use_global_device_ids=true, to_apply=%region_7.9 | all-reduce | flops 16 | bytes 128 | tf_op jit(solution)/shard_map/psum | solution.py:62
  420.7 21.3 %all_to_all.15 = bf16[16,16,2048]{2,1,0:T(8,128)(2,1)S(1)} all-to-all(bf16[16,16,2048]{2,1,0:T(8,128)(2,1)S(1)} %stack.7), channel_id=1, replica_groups=mesh['row'=8,'col'=16] {'col'}, dimensions={0} | all-to-all | bytes 2097152 | tf_op jit(solution)/shard_map/all_to_all | solution.py:67
  442.0 0.6 copy.41
  442.6 0.5 reshape_reshape.10
  443.2 0.7 copy.42
  443.8 0.8 gather_fusion.2
  444.6 3.9 fusion.21
  448.5 2.0 convolution_bitcast_fusion.2
  450.5 1.8 copy.44
  452.4 4.2 copy.80
  456.6 48.6 %reduce-scatter.10.cloned.1.call-done = f32[16,4096]{1,0:T(8,128)} async-done(((f32[16,32768]{1,0:T(8,128)}), f32[16,4096]{1,0:T(8,128)}) %reduce-scatter.10.cloned.1.call-update) | async-done | bytes 262160 | tf_op jit(solution)/shard_map/reduce_scatter | solution.py:87
  505.2 1.2 multiply_reduce_fusion.1
  506.4 64.6 %psum.45 = f32[16]{0:T(128)S(1)} all-reduce(f32[16]{0:T(128)S(1)} %multiply_reduce_fusion.1), channel_id=1, replica_groups=mesh['row'=8,'col'=16] {'row','col'}, use_global_device_ids=true, to_apply=%region_10.12 | all-reduce | flops 16 | bytes 128 | tf_op jit(solution)/shard_map/psum | solution.py:62
  571.0 1.7 fusion.83
  573.0 32.9 %all-gather.5.cloned.1.call-done = bf16[16,32768]{1,0:T(8,128)(2,1)} async-done(((bf16[16,4096]{1,0:T(8,128)(2,1)}), bf16[16,32768]{1,0:T(8,128)(2,1)}) %all-gather.5.cloned.1.call-update) | async-done | bytes 1048592 | tf_op jit(solution)/shard_map/all_gather | solution.py:96
  605.9 1.4 copy_bitcast_fusion.5
  607.3 0.8 gather_fusion.3
  608.1 5.5 fusion.24
  613.6 2.0 convolution_bitcast_fusion.1
  615.6 1.8 copy.47
  617.4 4.2 copy.79
  621.6 73.0 %reduce-scatter.12.cloned.1.call-done = f32[16,2048]{1,0:T(8,128)} async-done(((f32[16,32768]{1,0:T(8,128)}), f32[16,2048]{1,0:T(8,128)}) %reduce-scatter.12.cloned.1.call-update) | async-done | bytes 131088 | tf_op jit(solution)/shard_map/reduce_scatter | solution.py:99
  694.6 1.1 multiply_reduce_fusion.3
  695.7 66.4 %psum.46 = f32[16]{0:T(128)S(1)} all-reduce(f32[16]{0:T(128)S(1)} %get-tuple-element.15), channel_id=1, replica_groups=mesh['row'=8,'col'=16] {'row','col'}, use_global_device_ids=true, to_apply=%region_13.15 | all-reduce | flops 16 | bytes 128 | tf_op jit(solution)/shard_map/psum | solution.py:62
  762.4 21.0 %all_to_all.16 = bf16[16,16,2048]{2,1,0:T(8,128)(2,1)S(1)} all-to-all(bf16[16,16,2048]{2,1,0:T(8,128)(2,1)S(1)} %stack.8), channel_id=1, replica_groups=mesh['row'=8,'col'=16] {'col'}, dimensions={0} | all-to-all | bytes 2097152 | tf_op jit(solution)/shard_map/all_to_all | solution.py:67
  783.5 0.6 copy.48
  784.6 0.7 copy.49
  785.3 0.8 gather_fusion.4
  786.0 3.9 fusion.27
  789.9 2.0 convolution_bitcast_fusion
  791.9 1.8 copy.51
  793.8 4.2 copy.78
  797.9 48.7 %reduce-scatter.14.cloned.1.call-done = f32[16,4096]{1,0:T(8,128)} async-done(((f32[16,32768]{1,0:T(8,128)}), f32[16,4096]{1,0:T(8,128)}) %reduce-scatter.14.cloned.1.call-update) | async-done | bytes 262160 | tf_op jit(solution)/shard_map/reduce_scatter | solution.py:87
  846.7 1.2 multiply_reduce_fusion
  847.8 64.5 %psum.47 = f32[16]{0:T(128)S(1)} all-reduce(f32[16]{0:T(128)S(1)} %multiply_reduce_fusion), channel_id=1, replica_groups=mesh['row'=8,'col'=16] {'row','col'}, use_global_device_ids=true, to_apply=%region_16.18 | all-reduce | flops 16 | bytes 128 | tf_op jit(solution)/shard_map/psum | solution.py:62
  912.4 1.1 multiply_bitcast_fusion
  913.5 1.0 copy.53
  914.5 1.0 copy.52
  (41 shorter events, 2.4 us)
Async XLA Ops:
  7.2 77.4 %copy-start.3 = (s32[1,1,192]{2,1,0:T(1,128)S(1)}, s32[1,1,192]{2,1,0:T(1,128)}, u32[]{:S(2)}) copy-start(s32[1,1,192]{2,1,0:T(1,128)} %param.8) | copy-start | bytes 2308
  79.0 21.9 %all-to-all-start = ((bf16[16,16,2048]{2,1,0:T(8,128)(2,1)}), bf16[16,16,2048]{2,1,0:T(8,128)(2,1)S(1)}, u32[]{:S(2)}, u32[]{:S(2)}) async-start(bf16[16,16,2048]{2,1,0:T(8,128)(2,1)} %stack.6), calls=%async_computation | async-start | bytes 2097152 | tf_op jit(solution)/shard_map/all_to_all | solution.py:67
  83.8 79.9 %reduce-scatter.6.cloned.1.call-start = ((), (), s32[]{:S(2)}) async-start(), calls=%async_computation.8 | async-start | bytes 2359296 | tf_op jit(solution)/shard_map/reduce_scatter | solution.py:87
  103.5 3.9 copy-start.2
  115.4 148.8 %all-gather.3.cloned.1.call-start = ((), (), s32[]{:S(2)}) async-start(), calls=%async_computation.9 | async-start | bytes 1179648 | tf_op jit(solution)/shard_map/all_gather | solution.py:96
  231.1 121.9 %reduce-scatter.8.cloned.1.call-start = ((), (), s32[]{:S(2)}) async-start(), calls=%async_computation.10 | async-start | bytes 2228224 | tf_op jit(solution)/shard_map/reduce_scatter | solution.py:99
  279.9 73.1 %copy-start.1 = (f32[16,2048]{1,0:T(8,128)S(1)}, f32[16,2048]{1,0:T(8,128)}, u32[]{:S(2)}) copy-start(f32[16,2048]{1,0:T(8,128)} %param.11) | copy-start | bytes 393220
  279.9 225.3 %reduce-scatter.10.cloned.1.call-start = ((), (), s32[]{:S(2)}) async-start(), calls=%async_computation.11 | async-start | bytes 2359296 | tf_op jit(solution)/shard_map/reduce_scatter | solution.py:87
  456.5 48.7 %copy-start = (f32[16,4096]{1,0:T(8,128)S(1)}, f32[16,4096]{1,0:T(8,128)}, u32[]{:S(2)}) copy-start(f32[16,4096]{1,0:T(8,128)} %reduce-scatter.6.cloned.1.call-done) | copy-start | bytes 786436
  456.5 149.4 %all-gather.5.cloned.1.call-start = ((), (), s32[]{:S(2)}) async-start(), calls=%async_computation.12 | async-start | bytes 1179648 | tf_op jit(solution)/shard_map/all_gather | solution.py:96
  572.7 121.9 %reduce-scatter.12.cloned.1.call-start = ((), (), s32[]{:S(2)}) async-start(), calls=%async_computation.13 | async-start | bytes 2228224 | tf_op jit(solution)/shard_map/reduce_scatter | solution.py:99
  621.6 225.1 %reduce-scatter.14.cloned.1.call-start = ((), (), s32[]{:S(2)}) async-start(), calls=%async_computation.14 | async-start | bytes 2359296 | tf_op jit(solution)/shard_map/reduce_scatter | solution.py:87
Sparse Core Ops, SparseCore 0:
  115.5 48.1 reduce-scatter.5
  231.2 32.9 all-gather.2
  280.0 72.8 reduce-scatter.7
  456.7 48.5 reduce-scatter.9
  572.9 32.9 all-gather.4
  621.7 72.8 reduce-scatter.11
  798.1 48.5 reduce-scatter.13
